TPU v7x, 32 devices: a whole 2x2x4 slice. The times are simulated.
32 devices in a mesh: ctx: 8 (over y, x, core), chan: 4 (over z).
Axes of the slice: x: 2, y: 2, z: 4, core: 2. Of those that a mesh axis runs over, the one named last changes fastest.
Arguments:
- features: bfloat16 [3, 8192, 4096], P(None, 'chan', 'ctx'), may hold values from -6 to 6
- short_filter: float32 [3, 3, 8192], P(None, None, 'chan'), may hold values from -3.5 to 3.5
- lengths: int32 [8], P('ctx'), may hold values from 64 to 512, as said below
- offsets: int32 [8], P('ctx'), may hold values from 0 to 8128, as said below
- decay_rates: float32 [16, 1024], P(None, 'chan'), may hold values from 0 to 1, as said below
- residues: float32 [16, 1024], P(None, 'chan'), may hold values from -1 to 1
- skip_weight: float32 [8192], P('chan'), may hold values from -1 to 1
- out_weight: bfloat16 [8192, 4096], P('chan'), may hold values from -0.09375 to 0.09375
Outputs:
- projected: bfloat16 [4096, 4096], P('chan', 'ctx')
Inputs may be any that keep to these rules, and one draw needn't show every extreme that they name: `lengths`: used slots of each shard, counted from slot 0; some shard uses all 512 slots and some only 64. offsets[i] + lengths[i] <= offsets[i + 1]; the first offset is 0. `decay_rates`: positive rates.
All inputs are finite; a program needn't handle non-finite values.
Results may differ from a plain program's by a relative error of at most 0.018.
Values may be sent and summed in bfloat16 or wider, within the bound.
No kernel may reach another device: no remote copies, remote signals or barrier semaphores. Data moves between devices by JAX's collectives and lax.ppermute only.
A program may use at most 192 MiB of HBM per device.

v0:
```python
import jax
import jax.numpy as jnp
from jax import lax
from jax.sharding import PartitionSpec as P

highest = lax.Precision.HIGHEST


def passed_along(array, axis, by):
    length = lax.axis_size(axis)
    pairs = [(i, i + by) for i in range(length) if 0 <= i + by < length]
    return lax.ppermute(array, axis, pairs)


def shortened(array):
    return jax.tree.map(lambda a: a.astype(jnp.bfloat16) if a.dtype == jnp.float32 else a, array)


def block_pass(blocks, firsts, counts, decay_rows, residue):
    groups, per_group, block_count, block_width = blocks.shape
    mode_count = decay_rows.shape[0]
    rate_g = decay_rows.T
    residue_g = residue.T
    lag_index = jnp.arange(block_width)
    lag_float = lag_index.astype(jnp.float32)
    to_end = jnp.exp(-rate_g[:, None, :] * (block_width - 1.0 - lag_float)[None, :, None])
    raw_sums = lax.dot_general(
        blocks.reshape(groups, per_group * block_count, block_width),
        to_end,
        (((2,), (1,)), ((0,), (0,))),
        precision=highest,
    )
    lift = jnp.exp(rate_g[:, None, :] * (block_width - counts.astype(jnp.float32))[None, :, None])
    summary = raw_sums.reshape(groups, per_group, block_count, mode_count) * lift[:, None, :, :]
    difference = (lag_index[:, None] - lag_index[None, :]).astype(jnp.float32)
    distance = jnp.maximum(difference, 0.0)
    toeplitz = jnp.zeros((groups, block_width, block_width), jnp.float32)
    for mode_index in range(mode_count):
        toeplitz = toeplitz + residue_g[:, mode_index, None, None] * jnp.exp(
            -rate_g[:, mode_index, None, None] * distance[None]
        )
    toeplitz = jnp.where((difference >= 0.0)[None], toeplitz, 0.0)
    inner_part = lax.dot_general(blocks, toeplitz, (((3,), (2,)), ((0,), (0,))), precision=highest)
    lasts = firsts + counts.astype(jnp.float32) - 1.0
    gap_matrix = jnp.maximum(firsts[None, :] - lasts[:, None], 0.0)
    earlier_mask = lag_index[:block_count, None] < lag_index[None, :block_count]
    mixing = jnp.where(
        earlier_mask[None, None], jnp.exp(-rate_g[:, :, None, None] * gap_matrix[None, None]), 0.0
    )
    entering = jnp.einsum("gkcm,gmcb->gkbm", summary, mixing, precision=highest)
    return (inner_part, summary, entering, lasts)


def outer_pass(entering, decay_rows, residue, block_width):
    groups, per_group, block_count, mode_count = entering.shape
    rate_g = decay_rows.T
    lag_float = jnp.arange(block_width, dtype=jnp.float32)
    spread_values = residue.T[:, :, None] * jnp.exp(-rate_g[:, :, None] * lag_float[None, None, :])
    outer_part = lax.dot_general(
        entering.reshape(groups, per_group * block_count, mode_count),
        spread_values,
        (((2,), (1,)), ((0,), (0,))),
        precision=highest,
    )
    return outer_part.reshape(groups, per_group, block_count, block_width)


def shards(
    features, short_filter, lengths, offsets, decay_rates, residues, skip_weight, out_weight
):
    kernel_taps = short_filter.shape[1]
    channels = features.shape[1]
    slot_count = features.shape[2]
    groups = decay_rates.shape[1]
    per_group = channels // groups
    block_width = min(128, slot_count)
    length = lengths[0]
    tail_rows = lax.dynamic_slice_in_dim(
        features, length - (kernel_taps - 1), kernel_taps - 1, axis=2
    )
    previous = passed_along(tail_rows, "ctx", 1)
    extended = jnp.concatenate([previous, features], axis=2)
    short_conv = jnp.zeros((3, channels, slot_count), jnp.float32)
    for tap_index in range(kernel_taps):
        window_rows = lax.slice_in_dim(
            extended, kernel_taps - 1 - tap_index, kernel_taps - 1 - tap_index + slot_count, axis=2
        )
        short_conv = short_conv + short_filter[:, tap_index, :, None] * window_rows.astype(
            jnp.float32
        )
    usable = jnp.arange(slot_count) < length
    product = jnp.where(usable, short_conv[1] * short_conv[2], 0.0)
    all_lengths, all_offsets = (
        lax.all_gather(lengths, "ctx", axis=0, tiled=True),
        lax.all_gather(offsets, "ctx", axis=0, tiled=True),
    )
    ctx_count = lax.axis_size("ctx")
    rank_self = lax.axis_index("ctx")
    shared = groups // ctx_count
    decay_mine = lax.dynamic_slice_in_dim(decay_rates, rank_self * shared, shared, 1)
    residue_mine = lax.dynamic_slice_in_dim(residues, rank_self * shared, shared, 1)
    per_shard = slot_count // block_width
    within = jnp.tile(jnp.arange(per_shard) * block_width, ctx_count)
    firsts_all = jnp.repeat(all_offsets, per_shard).astype(jnp.float32) + within.astype(jnp.float32)
    counts_all = jnp.clip(jnp.repeat(all_lengths, per_shard) - within, 0, block_width)
    received = lax.all_to_all(
        product.reshape(groups, per_group, slot_count).astype(jnp.bfloat16),
        "ctx",
        split_axis=0,
        concat_axis=2,
        tiled=True,
    ).astype(jnp.float32)
    item_count = received.shape[1]
    blocks = received.reshape(shared, item_count, ctx_count * per_shard, block_width)
    inner_part, summary, entering, lasts = block_pass(
        blocks, firsts_all, counts_all, decay_mine, residue_mine
    )
    outer_part = outer_pass(entering, decay_mine, residue_mine, block_width)
    result = (inner_part + outer_part).reshape(shared, item_count, ctx_count * slot_count)
    long_conv = lax.all_to_all(
        shortened(result), "ctx", split_axis=2, concat_axis=0, tiled=True
    ).astype(result.dtype)
    long_conv = long_conv.reshape(channels, slot_count)
    mixed_rows = jnp.where(
        usable, short_conv[0] * (long_conv + skip_weight[:, None] * product), 0.0
    ).astype(jnp.bfloat16)
    return lax.psum_scatter(
        lax.dot_general(
            out_weight, mixed_rows, (((0,), (0,)), ((), ())), preferred_element_type=jnp.float32
        ).astype(jnp.bfloat16),
        "chan",
        scatter_dimension=0,
        tiled=True,
    )


def solution(mesh):
    placed = (
        P(None, "chan", "ctx"),
        P(None, None, "chan"),
        P("ctx"),
        P("ctx"),
        P(None, "chan"),
        P(None, "chan"),
        P("chan"),
        P("chan", None),
    )
    return jax.shard_map(
        shards, mesh=mesh, in_specs=placed, out_specs=P("chan", "ctx"), check_vma=False
    )
```

profile of v0, /device:TPU:0, one launch (start us, length us, event | category | flops | bytes accessed | tf_op | source)
XLA Modules:
  0.0 309.9 jit_solution(4460304330251844339)
XLA Ops:
  7.2 2.5 constant_dynamic-slice_fusion
  9.7 0.9 copy.54
  10.6 2.4 collective-permute-start
  13.6 0.6 dynamic-slice
  14.3 0.7 dynamic-update-slice.1
  15.0 0.7 dynamic-update-slice
  15.8 9.1 %all-reduce.2 = (s32[8]{0:T(128)S(1)}, s32[8]{0:T(128)S(1)}) all-reduce(s32[8]{0:T(128)S(1)} %dynamic-update-slice, s32[8]{0:T(128)S(1)} %dynamic-update-slice.1), channel_id=1, replica_groups=mesh['ctx'=8,'chan'=4] {'ctx'}, use_global_device_ids=true, to_apply=%add | all-reduce | flops 16 | bytes 128
  24.8 0.1 fusion.155
  24.9 0.1 clamp_convert_fusion
  24.9 0.1 broadcast_add_fusion
  25.1 0.9 copy.38
  26.0 12.5 %multiply_add_fusion = f32[3,2048,512]{2,1,0:T(8,128)S(1)} fusion(bf16[3,2048,512]{2,1,0:T(8,128)(2,1)} %param.8, bf16[3,2048,2]{2,1,0:T(8,128)(2,1)S(1)} %copy.38, f32[3,2048]{1,0:T(4,128)S(1)} %get-tuple-element.46, f32[3,2048]{1,0:T(4,128)S(1)} %get-tuple-element.47, f32[3,2048]{1,0:T(4,128)S(1)} %bitcast.143), kind=kLoop, calls=%fused_computation.1 | loop fusion | flops 44040192 | bytes 18972672 | tf_op jit(solution)/shard_map/add | solution.py:88
  38.5 4.5 %copy-done.2 = f32[3,2048,512]{2,1,0:T(8,128)} copy-done((f32[3,2048,512]{2,1,0:T(8,128)}, f32[3,2048,512]{2,1,0:T(8,128)S(1)}, u32[]{:S(2)}) %copy-start.2) | copy-done | bytes 12582936
  43.1 2.5 fusion.11
  45.5 3.7 %all-to-all-start = ((bf16[256,8,512]{2,1,0:T(8,128)(2,1)}), bf16[256,8,512]{2,1,0:T(8,128)(2,1)S(1)}, u32[]{:S(2)}, u32[]{:S(2)}) async-start(bf16[256,8,512]{2,1,0:T(8,128)(2,1)} %fusion.11), calls=%async_computation | async-start | bytes 4194304 | tf_op jit(solution)/shard_map/all_to_all | solution.py:106
  49.3 0.0 reduce-scatter.2.cloned.1.call-start
  49.3 0.1 dynamic-slice_bitcast_fusion.1
  49.4 0.1 convert_element_type.139
  49.5 0.1 add.115
  49.6 0.1 copy.44
  49.7 0.1 fusion.154
  49.7 0.1 copy.40
  49.8 0.1 copy.43
  50.0 0.1 broadcast_compare_fusion
  50.1 0.1 subtract_maximum_fusion
  50.2 0.1 multiply_exponential_fusion
  50.3 25.6 %all-to-all-done = bf16[256,8,512]{2,1,0:T(8,128)(2,1)S(1)} async-done(((bf16[256,8,512]{2,1,0:T(8,128)(2,1)}), bf16[256,8,512]{2,1,0:T(8,128)(2,1)S(1)}, u32[]{:S(2)}, u32[]{:S(2)}) %all-to-all-start) | async-done | bytes 2097184 | tf_op jit(solution)/shard_map/all_to_all | solution.py:106
  75.9 1.3 copy-done.3
  77.2 3.3 %copy.39 = bf16[32,8,8,512]{3,2,1,0:T(8,128)(2,1)S(1)} copy(bf16[32,8,8,512]{3,1,0,2:T(8,128)(2,1)} %bitcast.141) | data formatting | bytes 4194304 | tf_op jit(solution)/shard_map/all_to_all | solution.py:106
  80.5 2.8 reshape_reshape.3
  83.3 2.6 reshape.334
  85.9 3.4 %fusion.128 = f32[32,256,16]{1,2,0:T(8,128)S(1)} fusion(bf16[32,256,128]{2,1,0:T(8,128)(2,1)} %reshape_reshape.3, f32[128]{0:T(128)S(1)} %convert_subtract_fusion, f32[32,16]{1,0:T(8,128)S(1)} %copy.40), kind=kOutput, calls=%fused_computation.136 | convolution fusion | flops 201392128 | bytes 2624000 | tf_op jit(solution)/shard_map/dot_general | solution.py:27
  89.2 0.5 reshape.335
  89.7 17.6 %fusion.82 = f32[32,8,32,16]{2,1,3,0:T(8,128)} fusion(f32[32,8,32,16]{2,1,3,0:T(8,128)S(1)} %reshape.335, f32[32,32]{1,0:T(8,128)S(1)} %subtract_maximum_fusion, f32[32,16]{1,0:T(8,128)S(1)} %copy.40, pred[32,32]{1,0:T(8,128)(4,1)S(1)} %broadcast_compare_fusion, f32[32,32,16]{1,2,0:T(8,128)S(1)} %multiply_exponential_fusion), kind=kOutput, calls=%fused_computation.93 | convolution fusion | flops 51511296 | bytes 1121280 | tf_op jit(solution)/shard_map/gkcm,gmcb->gkbm/dot_general | solution.py:50
  107.3 2.1 reshape.336
  109.5 7.5 %fusion.123 = f32[32,256,128]{2,1,0:T(8,128)S(1)} fusion(f32[32,256,16]{1,2,0:T(8,128)S(1)} %reshape.336, f32[32,16]{1,0:T(8,128)S(1)} %copy.40, f32[32,16]{1,0:T(8,128)S(1)} %copy.44), kind=kOutput, calls=%fused_computation.130 | convolution fusion | flops 201457664 | bytes 4722688 | tf_op jit(solution)/shard_map/dot_general | solution.py:59
  117.0 9.5 %add_convert_fusion = bf16[32,8,32,128]{3,2,1,0:T(8,128)(2,1)S(1)} fusion(f32[32,8,32,128]{3,2,1,0:T(8,128)S(1)} %bitcast.142, bf16[32,8,32,128]{3,2,1,0:T(8,128)(2,1)S(1)} %copy-done.4, f32[32]{0:T(128)S(1)} %get-tuple-element.29, f32[32]{0:T(128)S(1)} %get-tuple-element.13, f32[32]{0:T(128)S(1)} %get-tuple-element.30, f32[32]{0:T(128)S(1)} %get-tuple-element.14, ...), kind=kOutput, calls=%fused_computation.22 | convolution fusion | flops 1637875712 | bytes 8474624 | tf_op jit(solution)/shard_map/dot_general | solution.py:43
  126.5 6.8 %copy.50 = bf16[32,8,32,128]{0,1,3,2:T(8,128)(2,1)} copy(bf16[32,8,32,128]{3,2,1,0:T(8,128)(2,1)S(1)} %add_convert_fusion) | data formatting | bytes 4194304 | tf_op jit(solution)/shard_map/convert_element_type | solution.py:16
  133.3 10.1 %reshape.351 = bf16[8,2,65536]{2,1,0:T(2,128)(2,1)S(1)} reshape(bf16[4096,8,32]{2,1,0:T(8,128)(2,1)} %bitcast.140) | data formatting | bytes 4194304
  143.5 29.8 %all_to_all.24 = bf16[8,2,65536]{2,1,0:T(2,128)(2,1)} all-to-all(bf16[8,2,65536]{2,1,0:T(2,128)(2,1)S(1)} %reshape.351), channel_id=1, replica_groups=mesh['ctx'=8,'chan'=4] {'ctx'}, dimensions={0} | all-to-all | bytes 4194304 | tf_op jit(solution)/shard_map/all_to_all | solution.py:120
  173.2 8.7 %reshape.352 = bf16[4096,8,32]{2,1,0:T(8,128)(2,1)} reshape(bf16[8,2,65536]{2,1,0:T(2,128)(2,1)} %all_to_all.24) | data formatting | bytes 4194304
  181.9 10.2 %convert_bitcast_fusion = f32[8,32,8,512]{1,2,3,0:T(8,128)} fusion(bf16[32,8,8,512]{0,1,3,2:T(8,128)(2,1)} %bitcast.139), kind=kLoop, calls=%fused_computation | loop fusion | flops 1048576 | bytes 6291456 | tf_op jit(solution)/shard_map/convert_element_type | solution.py:122
  192.1 12.0 %copy.47 = f32[8,32,8,512]{3,2,1,0:T(8,128)} copy(f32[8,32,8,512]{1,2,3,0:T(8,128)} %convert_bitcast_fusion) | data formatting | bytes 8388608 | tf_op jit(solution)/shard_map/convert_element_type | solution.py:122
  204.1 6.4 %fusion.8 = bf16[2048,512]{1,0:T(8,128)(2,1)S(1)} fusion(f32[3,2048,512]{2,1,0:T(8,128)} %copy-done.2, f32[8,32,8,512]{3,2,1,0:T(8,128)} %copy.47, f32[2048]{0:T(1024)S(1)} %copy-done.6, pred[512]{0:T(512)(128)(4,1)S(1)} %iota_compare_fusion), kind=kLoop, calls=%fused_computation.16 | loop fusion | flops 7340032 | bytes 18883072 | tf_op jit(solution)/shard_map/convert_element_type | solution.py:126
  210.5 14.0 %fusion.5 = bf16[4096,512]{0,1:T(8,128)(2,1)} fusion(bf16[2048,512]{1,0:T(8,128)(2,1)S(1)} %fusion.8, bf16[2048,4096]{1,0:T(8,128)(2,1)} %param.15), kind=kOutput, calls=%fused_computation.11 | convolution fusion | flops 8592031744 | bytes 23068672 | tf_op jit(solution)/shard_map/dot_general | solution.py:128
  224.5 0.0 reduce-scatter.2.cloned.1.call-update
  224.5 76.3 %reduce-scatter.2.cloned.1.call-done = bf16[1024,512]{0,1:T(8,128)(2,1)} async-done(((bf16[4096,512]{0,1:T(8,128)(2,1)}), bf16[1024,512]{0,1:T(8,128)(2,1)}) %reduce-scatter.2.cloned.1.call-update) | async-done | bytes 1048592 | tf_op jit(solution)/shard_map/reduce_scatter | solution.py:127
  300.8 2.3 copy.48
  (32 shorter events, 0.2 us)
Async XLA Ops:
  6.5 42.8 %copy-start = (f32[16,256]{1,0:T(8,128)S(1)}, f32[16,256]{1,0:T(8,128)}, u32[]{:S(2)}) copy-start(f32[16,256]{1,0:T(8,128)} %param.13) | copy-start | bytes 49156
  7.2 6.4 %copy-start.8 = (u32[32]{0:T(128)S(1)}, u32[32]{0:T(128)}, u32[]{:S(2)}) copy-start(u32[32]{0:T(128)} %constant.36) | copy-start | bytes 388
  7.2 17.6 %copy-start.5 = (f32[3,3,2048]{2,1,0:T(4,128)S(1)}, f32[3,3,2048]{2,1,0:T(4,128)}, u32[]{:S(2)}) copy-start(f32[3,3,2048]{2,1,0:T(4,128)} %param.9) | copy-start | bytes 221188
  10.6 14.5 %collective-permute-start = (bf16[3,2048,2]{1,0,2:T(4,128)(2,1)S(1)}, bf16[3,2048,2]{1,0,2:T(4,128)(2,1)S(1)}, u32[]{:S(2)}, u32[]{:S(2)}) collective-permute-start(bf16[3,2048,2]{1,0,2:T(4,128)(2,1)S(1)} %copy.54), channel_id=1, source_target_pairs={{0,4},{4,8},{8,12},{12,16},{16,20},{20,24},{24,28},{1,5},{5,9},{9,... | collective-permute-start | bytes 73736 | tf_op jit(solution)/shard_map/ppermute | solution.py:12
  38.5 4.5 %copy-start.2 = (f32[3,2048,512]{2,1,0:T(8,128)}, f32[3,2048,512]{2,1,0:T(8,128)S(1)}, u32[]{:S(2)}) copy-start(f32[3,2048,512]{2,1,0:T(8,128)S(1)} %multiply_add_fusion) | copy-start | bytes 37748740
  45.5 4.1 %copy-start.7 = (f32[16,256]{1,0:T(8,128)S(1)}, f32[16,256]{1,0:T(8,128)}, u32[]{:S(2)}) copy-start(f32[16,256]{1,0:T(8,128)} %param.12) | copy-start | bytes 49156
  45.5 30.3 %all-to-all-start = ((bf16[256,8,512]{2,1,0:T(8,128)(2,1)}), bf16[256,8,512]{2,1,0:T(8,128)(2,1)S(1)}, u32[]{:S(2)}, u32[]{:S(2)}) async-start(bf16[256,8,512]{2,1,0:T(8,128)(2,1)} %fusion.11), calls=%async_computation | async-start | bytes 4194304 | tf_op jit(solution)/shard_map/all_to_all | solution.py:106
  49.3 251.5 %reduce-scatter.2.cloned.1.call-start = ((), (), s32[]{:S(2)}) async-start(), calls=%async_computation.3 | async-start | bytes 5242880 | tf_op jit(solution)/shard_map/reduce_scatter | solution.py:127
  75.9 1.3 copy-start.3
  109.5 7.5 %copy-start.4 = (bf16[32,8,32,128]{3,2,1,0:T(8,128)(2,1)S(1)}, bf16[32,8,32,128]{3,2,1,0:T(8,128)(2,1)}, u32[]{:S(2)}) copy-start(bf16[32,8,32,128]{3,2,1,0:T(8,128)(2,1)} %reshape.334) | copy-start | bytes 6291460
  192.1 12.0 %copy-start.6 = (f32[2048]{0:T(1024)S(1)}, f32[2048]{0:T(1024)}, u32[]{:S(2)}) copy-start(f32[2048]{0:T(1024)} %param.14) | copy-start | bytes 24580
  224.5 78.6 %copy-start.1 = (f32[16,256]{1,0:T(8,128)S(1)}, f32[16,256]{1,0:T(8,128)}, u32[]{:S(2)}) copy-start(f32[16,256]{1,0:T(8,128)} %param.13) | copy-start | bytes 49156
Sparse Core Ops, SparseCore 0:
  224.6 76.1 reduce-scatter.1
where the time goes:
time: 311 us; the launch traced here: 310 us
  waiting for transfers between devices  102 us (33%)
  local copies, waits for them, and re-layouts  63.9 us (21%)
  matrix products  52 us (17%)
  blocking collectives  38.8 us (12%)
  other arithmetic  32.2 us (10%)
  between operations  15 us (5%)
  starting transfers between devices  6.13 us (2%)
    reduce_scatter x1, waiting for transfers between devices, shards(): lax.psum_scatter(lax.dot_general(out_weight, mixed_rows, (((0,), (0,)), (...  76.3 us
    all_to_all x1, blocking collectives, shards(): lax.all_to_all(shortened(result), 'ctx', split_axis=2, concat_axis=0, til...  29.8 us
    unnamed x28, local copies, waits for them, and re-layouts  27.7 us
    all_to_all x1, waiting for transfers between devices, shards(): lax.all_to_all(product.reshape(groups, per_group, slot_count).astype(jnp....  25.6 us
    dot_general x1, matrix products, block_pass(): entering = jnp.einsum('gkcm,gmcb->gkbm', summary, mixing, precision=highest)  17.6 us
    dot_general x1, matrix products, shards(): lax.dot_general(out_weight, mixed_rows, (((0,), (0,)), ((), ())), preferr...  14 us
    add x1, other arithmetic, shards(): short_conv + short_filter[:, tap_index, :, None] * window_rows.astype(jnp...  12.5 us
    convert_element_type x1, local copies, waits for them, and re-layouts, shards(): long_conv = lax.all_to_all(shortened(result), 'ctx', split_axis=2, concat...  12 us
  transfers between devices with their start and end apart: 3, of which 2 were waited for; matrix products, arithmetic and copies ran while one was open for 1% of the time, Pallas kernels for 0%

commit v1 on v0

--- a/solution.py
+++ b/solution.py
@@ -4,6 +4,29 @@
 from jax.sharding import PartitionSpec as P
 
 highest = lax.Precision.HIGHEST
+
+
+def split_up(x, dim, size):
+    shape = x.shape
+    blocks = x.reshape(*shape[:dim], size, shape[dim] // size, *shape[dim + 1 :])
+    return jnp.moveaxis(blocks, dim, 0)
+
+
+def joined_along(parts, dim):
+    parts = jnp.moveaxis(parts, 0, dim)
+    lengths = parts.shape
+    return parts.reshape(*lengths[:dim], lengths[dim] * lengths[dim + 1], *lengths[dim + 2 :])
+
+
+def exchange_in_pairs(array, axis, split_dim, concat_dim):
+    size, position = (lax.axis_size(axis), lax.axis_index(axis))
+    blocks = split_up(array, split_dim, size)
+    outs = [blocks[position]]
+    for lap in range(1, size):
+        sent = blocks[position ^ lap]
+        outs.append(lax.ppermute(sent, axis, [(i, i ^ lap) for i in range(size)]))
+    blocks = jnp.stack(outs)[position ^ jnp.arange(size)]
+    return joined_along(blocks, concat_dim)
 
 
 def passed_along(array, axis, by):
@@ -117,9 +140,7 @@
     )
     outer_part = outer_pass(entering, decay_mine, residue_mine, block_width)
     result = (inner_part + outer_part).reshape(shared, item_count, ctx_count * slot_count)
-    long_conv = lax.all_to_all(
-        shortened(result), "ctx", split_axis=2, concat_axis=0, tiled=True
-    ).astype(result.dtype)
+    long_conv = exchange_in_pairs(shortened(result), "ctx", 2, 0).astype(result.dtype)
     long_conv = long_conv.reshape(channels, slot_count)
     mixed_rows = jnp.where(
         usable, short_conv[0] * (long_conv + skip_weight[:, None] * product), 0.0

time: 311 us -> 270 us (0.87)
  blocking collectives: 38.8 us -> 9.05 us
  local copies, waits for them, and re-layouts: 63.9 us -> 37.4 us
  waiting for transfers between devices: 102 us -> 124 us
  other arithmetic: 32.2 us -> 15.7 us
  matrix products: 52 us -> 57.9 us
  starting transfers between devices: 6.13 us -> 10.5 us
    all_to_all x1 -> x0, blocking collectives: 29.8 us -> none  [shards(): lax.all_to_all(shortened(result), 'ctx', split_axis=2, concat_axis=0, til...]
    ppermute x0 -> x7, waiting for transfers between devices: none -> 22.1 us  [exchange_in_pairs(): outs.append(lax.ppermute(sent, axis, [(i, i ^ lap) for i in range(size)]))]
    unnamed x28 -> x40, local copies, waits for them, and re-layouts: 27.7 us -> 9.26 us
    convert_element_type x2 -> x0, other arithmetic: 16.6 us -> none  [the longest x1 10.2 us: shards(): long_conv = lax.all_to_all(shortened(result), 'ctx', split_axis=2, concat...]
    convert_element_type x1 -> x0, local copies, waits for them, and re-layouts: 12 us -> none  [shards(): long_conv = lax.all_to_all(shortened(result), 'ctx', split_axis=2, concat...]
    dot_general x1, matrix products: 14 us -> 19.7 us  [shards(): lax.dot_general(out_weight, mixed_rows, (((0,), (0,)), ((), ())), preferr...]
    another operation x0 -> x2, local copies, waits for them, and re-layouts: none -> 5.55 us
    ppermute x0 -> x7, starting transfers between devices: none -> 4.49 us  [exchange_in_pairs(): outs.append(lax.ppermute(sent, axis, [(i, i ^ lap) for i in range(size)]))]
  transfers between devices with their start and end apart: 3 -> 10, of which waited for: 2 -> 5; matrix products, arithmetic and copies ran while one was open for 1% -> 1% of each run, Pallas kernels for 0% -> 0%
where the time goes in v1:
time: 270 us
  waiting for transfers between devices  124 us (46%)
  matrix products  57.9 us (21%)
  local copies, waits for them, and re-layouts  37.4 us (14%)
  other arithmetic  15.7 us (6%)
  between operations  15.1 us (6%)
  starting transfers between devices  10.5 us (4%)
  blocking collectives  9.05 us (3%)
    reduce_scatter x1, waiting for transfers between devices, shards(): lax.psum_scatter(lax.dot_general(out_weight, mixed_rows, (((0,), (0,)), (...  76.4 us
    all_to_all x1, waiting for transfers between devices, shards(): lax.all_to_all(product.reshape(groups, per_group, slot_count).astype(jnp....  25.6 us
    ppermute x7, waiting for transfers between devices, exchange_in_pairs(): outs.append(lax.ppermute(sent, axis, [(i, i ^ lap) for i in range(size)]))  22.1 us
    dot_general x1, matrix products, shards(): lax.dot_general(out_weight, mixed_rows, (((0,), (0,)), ((), ())), preferr...  19.7 us
    dot_general x1, matrix products, block_pass(): entering = jnp.einsum('gkcm,gmcb->gkbm', summary, mixing, precision=highest)  17.7 us
    add x1, other arithmetic, shards(): short_conv + short_filter[:, tap_index, :, None] * window_rows.astype(jnp...  12.6 us
    dot_general x1, matrix products, block_pass(): lax.dot_general(blocks, toeplitz, (((3,), (2,)), ((0,), (0,))), precision...  9.67 us
    unnamed x40, local copies, waits for them, and re-layouts  9.26 us
  transfers between devices with their start and end apart: 10, of which 5 were waited for; matrix products, arithmetic and copies ran while one was open for 1% of the time, Pallas kernels for 0%

profile of v1, /device:TPU:0, one launch (start us, length us, event | category | flops | bytes accessed | tf_op | source)
XLA Modules:
  0.0 269.8 jit_solution(15902761827236050118)
XLA Ops:
  7.2 2.5 constant_dynamic-slice_fusion.8
  9.7 0.9 copy.53
  10.6 2.4 collective-permute-start
  13.8 0.6 dynamic-slice.32
  14.3 0.7 dynamic-update-slice.1
  15.1 0.7 dynamic-update-slice
  15.8 9.1 %all-reduce.2 = (s32[8]{0:T(128)S(1)}, s32[8]{0:T(128)S(1)}) all-reduce(s32[8]{0:T(128)S(1)} %dynamic-update-slice, s32[8]{0:T(128)S(1)} %dynamic-update-slice.1), channel_id=1, replica_groups=mesh['ctx'=8,'chan'=4] {'ctx'}, use_global_device_ids=true, to_apply=%add | all-reduce | flops 16 | bytes 128
  24.9 0.1 fusion.160
  25.1 0.1 clamp_convert_fusion
  25.2 0.9 copy.32
  26.1 12.6 %multiply_add_fusion = f32[3,2048,512]{2,1,0:T(8,128)S(1)} fusion(bf16[3,2048,512]{2,1,0:T(8,128)(2,1)} %param.8, bf16[3,2048,2]{2,1,0:T(8,128)(2,1)S(1)} %copy.32, f32[3,2048]{1,0:T(4,128)S(1)} %get-tuple-element.54, f32[3,2048]{1,0:T(4,128)S(1)} %get-tuple-element.55, f32[3,2048]{1,0:T(4,128)S(1)} %bitcast.184), kind=kLoop, calls=%fused_computation.1 | loop fusion | flops 44040192 | bytes 18972672 | tf_op jit(solution)/shard_map/add | solution.py:111
  38.7 4.5 %copy-done.2 = f32[3,2048,512]{2,1,0:T(8,128)} copy-done((f32[3,2048,512]{2,1,0:T(8,128)}, f32[3,2048,512]{2,1,0:T(8,128)S(1)}, u32[]{:S(2)}) %copy-start.2) | copy-done | bytes 12582936
  43.2 2.5 fusion.10
  45.7 3.6 %all-to-all-start = ((bf16[256,8,512]{2,1,0:T(8,128)(2,1)}), bf16[256,8,512]{2,1,0:T(8,128)(2,1)S(1)}, u32[]{:S(2)}, u32[]{:S(2)}) async-start(bf16[256,8,512]{2,1,0:T(8,128)(2,1)} %fusion.10), calls=%async_computation | async-start | bytes 4194304 | tf_op jit(solution)/shard_map/all_to_all | solution.py:129
  49.3 0.1 dynamic-slice_bitcast_fusion.1
  49.4 0.1 copy.34
  49.5 0.1 copy.37
  49.6 0.1 add.149
  49.7 0.1 convert_element_type.134
  49.7 0.1 copy.38
  49.9 0.1 broadcast_compare_fusion
  50.0 0.1 subtract_maximum_fusion
  50.1 0.1 multiply_exponential_fusion
  50.2 25.6 %all-to-all-done = bf16[256,8,512]{2,1,0:T(8,128)(2,1)S(1)} async-done(((bf16[256,8,512]{2,1,0:T(8,128)(2,1)}), bf16[256,8,512]{2,1,0:T(8,128)(2,1)S(1)}, u32[]{:S(2)}, u32[]{:S(2)}) %all-to-all-start) | async-done | bytes 2097184 | tf_op jit(solution)/shard_map/all_to_all | solution.py:129
  75.9 1.3 copy-done.3
  77.2 3.3 %copy.33 = bf16[32,8,8,512]{3,2,1,0:T(8,128)(2,1)S(1)} copy(bf16[32,8,8,512]{3,1,0,2:T(8,128)(2,1)} %bitcast.174) | data formatting | bytes 4194304 | tf_op jit(solution)/shard_map/all_to_all | solution.py:129
  80.5 2.8 %reshape_reshape.3 = bf16[32,256,128]{2,1,0:T(8,128)(2,1)} reshape(bf16[32,8,8,512]{3,2,1,0:T(8,128)(2,1)S(1)} %copy.33) | data formatting | bytes 4194304 | tf_op jit(solution)/shard_map/reshape;reshape | solution.py:51
  83.2 2.6 reshape.366
  85.9 3.4 %fusion.132 = f32[32,256,16]{1,2,0:T(8,128)S(1)} fusion(bf16[32,256,128]{2,1,0:T(8,128)(2,1)} %reshape_reshape.3, f32[128]{0:T(128)S(1)} %convert_subtract_fusion, f32[32,16]{1,0:T(8,128)S(1)} %copy.34), kind=kOutput, calls=%fused_computation.155 | convolution fusion | flops 201392128 | bytes 2624000 | tf_op jit(solution)/shard_map/dot_general | solution.py:50
  89.2 0.5 reshape.367
  89.7 17.7 %fusion.85 = f32[32,8,32,16]{2,1,3,0:T(8,128)} fusion(f32[32,8,32,16]{2,1,3,0:T(8,128)S(1)} %reshape.367, f32[32,32]{1,0:T(8,128)S(1)} %subtract_maximum_fusion, f32[32,16]{1,0:T(8,128)S(1)} %copy.34, pred[32,32]{1,0:T(8,128)(4,1)S(1)} %broadcast_compare_fusion, f32[32,32,16]{1,2,0:T(8,128)S(1)} %multiply_exponential_fusion), kind=kOutput, calls=%fused_computation.96 | convolution fusion | flops 51511296 | bytes 1121280 | tf_op jit(solution)/shard_map/gkcm,gmcb->gkbm/dot_general | solution.py:73
  107.4 2.1 reshape.368
  109.5 7.5 %fusion.127 = f32[32,256,128]{2,1,0:T(8,128)S(1)} fusion(f32[32,256,16]{1,2,0:T(8,128)S(1)} %reshape.368, f32[32,16]{1,0:T(8,128)S(1)} %copy.34, f32[32,16]{1,0:T(8,128)S(1)} %copy.38), kind=kOutput, calls=%fused_computation.149 | convolution fusion | flops 201457664 | bytes 4722688 | tf_op jit(solution)/shard_map/dot_general | solution.py:82
  117.1 9.7 %add_convert_fusion = bf16[32,8,32,128]{3,2,1,0:T(8,128)(2,1)} fusion(f32[32,8,32,128]{3,2,1,0:T(8,128)S(1)} %bitcast.175, bf16[32,8,32,128]{3,2,1,0:T(8,128)(2,1)S(1)} %copy-done.4, f32[32]{0:T(128)S(1)} %get-tuple-element.37, f32[32]{0:T(128)S(1)} %get-tuple-element.21, f32[32]{0:T(128)S(1)} %get-tuple-element.38, f32[32]{0:T(128)S(1)} %get-tuple-element.22, ...), kind=kOutput, calls=%fused_computation.22 | convolution fusion | flops 1637875712 | bytes 8474624 | tf_op jit(solution)/shard_map/dot_general | solution.py:66
  126.7 3.1 %convert_element_type.137 = bf16[32,8,8,512]{3,2,1,0:T(8,128)(2,1)S(1)} reshape(bf16[32,8,32,128]{3,2,1,0:T(8,128)(2,1)} %add_convert_fusion) | data formatting | bytes 4194304 | tf_op jit(solution)/shard_map/convert_element_type | solution.py:39
  129.8 5.5 %constant_dynamic-slice_fusion = (bf16[32,8,1,512]{3,2,1,0:T(2,128)(2,1)S(1)}, bf16[32,8,1,512]{3,2,1,0:T(2,128)(2,1)S(1)}, bf16[32,8,1,512]{3,2,1,0:T(2,128)(2,...) fusion(bf16[32,8,8,512]{3,2,1,0:T(8,128)(2,1)S(1)} %convert_ele, ...), kind=kLoop, calls=%fused_computation.175 | loop fusion | bytes 4194336 | tf_op jit(solution)/shard_map/dynamic-slice.7
  135.5 0.6 collective-permute-start.2
  136.2 1.4 collective-permute-start.3
  137.6 0.6 collective-permute-start.4
  138.3 1.2 collective-permute-start.5
  139.6 0.7 collective-permute-start.6
  140.2 4.5 %collective-permute-done.2 = bf16[32,8,512]{2,1,0:T(8,128)(2,1)S(1)} collective-permute-done((bf16[32,8,512]{2,1,0:T(8,128)(2,1)S(1)}, bf16[32,8,512]{2,1,0:T(8,128)(2,1)S(1)}, u32[]{:S(2)}, u32[]{:S(2)}) %collective-permute-start.2) | collective-permute-done | bytes 262176 | tf_op jit(solution)/shard_map/ppermute | solution.py:27
  144.7 4.8 %collective-permute-done.3 = bf16[32,8,512]{2,1,0:T(8,128)(2,1)S(1)} collective-permute-done((bf16[32,8,512]{2,1,0:T(8,128)(2,1)S(1)}, bf16[32,8,512]{2,1,0:T(8,128)(2,1)S(1)}, u32[]{:S(2)}, u32[]{:S(2)}) %collective-permute-start.3) | collective-permute-done | bytes 262176 | tf_op jit(solution)/shard_map/ppermute | solution.py:27
  149.6 12.9 %collective-permute-done.5 = bf16[32,8,512]{2,1,0:T(8,128)(2,1)S(1)} collective-permute-done((bf16[32,8,512]{2,1,0:T(8,128)(2,1)S(1)}, bf16[32,8,512]{2,1,0:T(8,128)(2,1)S(1)}, u32[]{:S(2)}, u32[]{:S(2)}) %collective-permute-start.5) | collective-permute-done | bytes 262176 | tf_op jit(solution)/shard_map/ppermute | solution.py:27
  162.6 2.0 gather_fusion
  164.6 19.7 %fusion.5 = bf16[4096,512]{0,1:T(8,128)(2,1)} fusion(bf16[2048,4096]{1,0:T(8,128)(2,1)} %param.15, f32[3,2048,512]{2,1,0:T(8,128)} %copy-done.2, bf16[2048,512]{1,0:T(8,128)(2,1)} %bitcast.176, f32[2048]{0:T(1024)S(1)} %copy-done.7, pred[512]{0:T(512)(128)(4,1)S(1)} %iota_compare_fusion), kind=kOutput, calls=%fused_computation.11 | convolution fusion | flops 8600420352 | bytes 35660288 | tf_op jit(solution)/shard_map/dot_general | solution.py:149
  184.3 76.4 %reduce-scatter.2.cloned.1.call-done = bf16[1024,512]{0,1:T(8,128)(2,1)} async-done(((bf16[4096,512]{0,1:T(8,128)(2,1)}), bf16[1024,512]{0,1:T(8,128)(2,1)}) %reduce-scatter.2.cloned.1.call-update) | async-done | bytes 1048592 | tf_op jit(solution)/shard_map/reduce_scatter | solution.py:148
  260.7 2.3 copy.48
  (59 shorter events, 0.9 us)
Async XLA Ops:
  6.5 42.8 %copy-start = (f32[16,256]{1,0:T(8,128)S(1)}, f32[16,256]{1,0:T(8,128)}, u32[]{:S(2)}) copy-start(f32[16,256]{1,0:T(8,128)} %param.13) | copy-start | bytes 49156
  7.2 5.8 %copy-start.5 = (f32[3,3,2048]{2,1,0:T(4,128)S(1)}, f32[3,3,2048]{2,1,0:T(4,128)}, u32[]{:S(2)}) copy-start(f32[3,3,2048]{2,1,0:T(4,128)} %param.9) | copy-start | bytes 221188
  7.2 6.5 %copy-start.8 = (u32[32]{0:T(128)S(1)}, u32[32]{0:T(128)}, u32[]{:S(2)}) copy-start(u32[32]{0:T(128)} %constant.53) | copy-start | bytes 388
  7.2 17.7 %copy-start.6 = (f32[16,256]{1,0:T(8,128)S(1)}, f32[16,256]{1,0:T(8,128)}, u32[]{:S(2)}) copy-start(f32[16,256]{1,0:T(8,128)} %param.12) | copy-start | bytes 49156
  10.6 14.5 %collective-permute-start = (bf16[3,2048,2]{1,0,2:T(4,128)(2,1)S(1)}, bf16[3,2048,2]{1,0,2:T(4,128)(2,1)S(1)}, u32[]{:S(2)}, u32[]{:S(2)}) collective-permute-start(bf16[3,2048,2]{1,0,2:T(4,128)(2,1)S(1)} %copy.53), channel_id=1, source_target_pairs={{0,4},{4,8},{8,12},{12,16},{16,20},{20,24},{24,28},{1,5},{5,9},{9,... | collective-permute-start | bytes 73736 | tf_op jit(solution)/shard_map/ppermute | solution.py:35
  38.7 4.5 %copy-start.2 = (f32[3,2048,512]{2,1,0:T(8,128)}, f32[3,2048,512]{2,1,0:T(8,128)S(1)}, u32[]{:S(2)}) copy-start(f32[3,2048,512]{2,1,0:T(8,128)S(1)} %multiply_add_fusion) | copy-start | bytes 37748740
  45.7 30.2 %all-to-all-start = ((bf16[256,8,512]{2,1,0:T(8,128)(2,1)}), bf16[256,8,512]{2,1,0:T(8,128)(2,1)S(1)}, u32[]{:S(2)}, u32[]{:S(2)}) async-start(bf16[256,8,512]{2,1,0:T(8,128)(2,1)} %fusion.10), calls=%async_computation | async-start | bytes 4194304 | tf_op jit(solution)/shard_map/all_to_all | solution.py:129
  49.3 211.4 %reduce-scatter.2.cloned.1.call-start = ((), (), s32[]{:S(2)}) async-start(), calls=%async_computation.2 | async-start | bytes 5242880 | tf_op jit(solution)/shard_map/reduce_scatter | solution.py:148
  75.9 1.3 copy-start.3
  109.5 7.5 %copy-start.4 = (bf16[32,8,32,128]{3,2,1,0:T(8,128)(2,1)S(1)}, bf16[32,8,32,128]{3,2,1,0:T(8,128)(2,1)}, u32[]{:S(2)}) copy-start(bf16[32,8,32,128]{3,2,1,0:T(8,128)(2,1)} %reshape.366) | copy-start | bytes 6291460
  135.4 4.1 %collective-permute-start.1 = (bf16[32,8,512]{2,1,0:T(8,128)(2,1)S(1)}, bf16[32,8,512]{2,1,0:T(8,128)(2,1)S(1)}, u32[]{:S(2)}, u32[]{:S(2)}) collective-permute-start(bf16[32,8,512]{2,1,0:T(8,128)(2,1)S(1)} %bitcast.183), channel_id=1, source_target_pairs={{0,4},{4,0},{8,12},{12,8},{16,20},{20,16},{24,28},{28,24},{1,5},{5... | collective-permute-start | bytes 786440 | tf_op jit(solution)/shard_map/ppermute | solution.py:27
  135.5 9.2 %collective-permute-start.2 = (bf16[32,8,512]{2,1,0:T(8,128)(2,1)S(1)}, bf16[32,8,512]{2,1,0:T(8,128)(2,1)S(1)}, u32[]{:S(2)}, u32[]{:S(2)}) collective-permute-start(bf16[32,8,512]{2,1,0:T(8,128)(2,1)S(1)} %bitcast.182), channel_id=1, source_target_pairs={{0,8},{4,12},{8,0},{12,4},{16,24},{20,28},{24,16},{28,20},{1,9},{5... | collective-permute-start | bytes 786440 | tf_op jit(solution)/shard_map/ppermute | solution.py:27
  136.2 13.3 %collective-permute-start.3 = (bf16[32,8,512]{2,1,0:T(8,128)(2,1)S(1)}, bf16[32,8,512]{2,1,0:T(8,128)(2,1)S(1)}, u32[]{:S(2)}, u32[]{:S(2)}) collective-permute-start(bf16[32,8,512]{2,1,0:T(8,128)(2,1)S(1)} %bitcast.181), channel_id=1, source_target_pairs={{0,12},{4,8},{8,4},{12,0},{16,28},{20,24},{24,20},{28,16},{1,13},{... | collective-permute-start | bytes 786440 | tf_op jit(solution)/shard_map/ppermute | solution.py:27
  137.6 11.9 %collective-permute-start.4 = (bf16[32,8,512]{2,1,0:T(8,128)(2,1)S(1)}, bf16[32,8,512]{2,1,0:T(8,128)(2,1)S(1)}, u32[]{:S(2)}, u32[]{:S(2)}) collective-permute-start(bf16[32,8,512]{2,1,0:T(8,128)(2,1)S(1)} %bitcast.180), channel_id=1, source_target_pairs={{0,16},{4,20},{8,24},{12,28},{16,0},{20,4},{24,8},{28,12},{1,17},{... | collective-permute-start | bytes 786440 | tf_op jit(solution)/shard_map/ppermute | solution.py:27
  138.3 24.2 %collective-permute-start.5 = (bf16[32,8,512]{2,1,0:T(8,128)(2,1)S(1)}, bf16[32,8,512]{2,1,0:T(8,128)(2,1)S(1)}, u32[]{:S(2)}, u32[]{:S(2)}) collective-permute-start(bf16[32,8,512]{2,1,0:T(8,128)(2,1)S(1)} %bitcast.179), channel_id=1, source_target_pairs={{0,20},{4,16},{8,28},{12,24},{16,4},{20,0},{24,12},{28,8},{1,21},{... | collective-permute-start | bytes 786440 | tf_op jit(solution)/shard_map/ppermute | solution.py:27
  139.6 22.9 %collective-permute-start.6 = (bf16[32,8,512]{2,1,0:T(8,128)(2,1)S(1)}, bf16[32,8,512]{2,1,0:T(8,128)(2,1)S(1)}, u32[]{:S(2)}, u32[]{:S(2)}) collective-permute-start(bf16[32,8,512]{2,1,0:T(8,128)(2,1)S(1)} %bitcast.178), channel_id=1, source_target_pairs={{0,24},{4,28},{8,16},{12,20},{16,8},{20,12},{24,0},{28,4},{1,25},{... | collective-permute-start | bytes 786440 | tf_op jit(solution)/shard_map/ppermute | solution.py:27
  144.7 17.8 %collective-permute-start.7 = (bf16[32,8,512]{2,1,0:T(8,128)(2,1)S(1)}, bf16[32,8,512]{2,1,0:T(8,128)(2,1)S(1)}, u32[]{:S(2)}, u32[]{:S(2)}) collective-permute-start(bf16[32,8,512]{2,1,0:T(8,128)(2,1)S(1)} %bitcast.177), channel_id=1, source_target_pairs={{0,28},{4,24},{8,20},{12,16},{16,12},{20,8},{24,4},{28,0},{1,29},{... | collective-permute-start | bytes 786440 | tf_op jit(solution)/shard_map/ppermute | solution.py:27
  162.6 2.0 copy-start.7
  184.3 78.7 %copy-start.1 = (f32[16,256]{1,0:T(8,128)S(1)}, f32[16,256]{1,0:T(8,128)}, u32[]{:S(2)}) copy-start(f32[16,256]{1,0:T(8,128)} %param.13) | copy-start | bytes 49156
Sparse Core Ops, SparseCore 0:
  184.4 76.2 reduce-scatter.1
